TPU v7x, 32 devices: a whole 2x2x4 slice. The times are simulated.
32 devices in a mesh: dp: 2 (over y), ctx: 4 (over z), fsdp: 4 (over x, core).
Axes of the slice: x: 2, y: 2, z: 4, core: 2. Of those that a mesh axis runs over, the one named last changes fastest.
Arguments:
- layer_input: bfloat16 [8, 2048, 768], P(('dp', 'fsdp'), 'ctx'), may hold values from -6 to 6
- first_values: bfloat16 [8, 2048, 384], P(('dp', 'fsdp'), 'ctx'), may hold values from -6 to 6
- segment_ids: int32 [8, 2048], P(('dp', 'fsdp')), may hold values from 0 to 7, never falling along the last dimension, each value on 1 to 1024 neighbouring positions
- pairing: int32 [8], replicated, may hold values from 0 to 7, as said below
- norm_gains: bfloat16 [2, 768], P(None, 'fsdp'), may hold values from 0.099609375 to 1.8984375
- norm_biases: bfloat16 [2, 768], P(None, 'fsdp'), may hold values from -2 to 2
- w_qkv: bfloat16 [768, 1920], P('fsdp'), may hold values from -0.21875 to 0.21875
- w_out: bfloat16 [768, 768], P('fsdp'), may hold values from -0.875 to 0.875
- w_up: bfloat16 [768, 3072], P(None, 'fsdp'), may hold values from -0.21875 to 0.21875
- w_down: bfloat16 [3072, 768], P('fsdp'), may hold values from -0.109375 to 0.109375
- cotangent: bfloat16 [8, 2048, 768], P(('dp', 'fsdp'), 'ctx'), may hold values from -6 to 6
Outputs:
- layer_out: bfloat16 [8, 2048, 768], P(('dp', 'fsdp'), 'ctx')
- input_grad: float32 [8, 2048, 768], P(('dp', 'fsdp'), 'ctx')
- first_values_grad: float32 [8, 2048, 384], P(('dp', 'fsdp'), 'ctx')
- gains_grad: float32 [2, 768], P(None, 'fsdp')
- biases_grad: float32 [2, 768], P(None, 'fsdp')
- qkv_grad: float32 [768, 1920], P('fsdp')
- out_grad: float32 [768, 768], P('fsdp')
- up_grad: float32 [768, 3072], P(None, 'fsdp')
- down_grad: float32 [3072, 768], P('fsdp')
Inputs may be any that keep to these rules, and one draw needn't show every extreme that they name: `segment_ids`: along each sequence the ids never fall; each document holds 1 to 1024 positions, one exactly that many. `pairing`: every block is named once; entries 2c and 2c + 1 name blocks b and 7 - b for some b, in either order.
All inputs are finite; a program needn't handle non-finite values.
Results may differ from a plain program's by a relative error of at most 0.019.
Values may be sent and summed in bfloat16 or wider, within the bound.
No kernel may reach another device: no remote copies, remote signals or barrier semaphores. Data moves between devices by JAX's collectives and lax.ppermute only.
A program may use at most 192 MiB of HBM per device.

v0:
```python
import jax
import jax.numpy as jnp
from jax import lax
from jax.sharding import PartitionSpec as P

D = 768
HEADS = 12
HD = 64
VH = 6
EPSILON = 1e-05
NEGATIVE = -1e30


def norm_layer(values_in, gain, bias):
    center = jnp.mean(values_in, axis=-1, keepdims=True)
    centred = values_in - center
    spread = jnp.mean(centred * centred, axis=-1, keepdims=True)
    return centred * lax.rsqrt(spread + EPSILON) * gain + bias


def gelu_tanh(values_in):
    return jax.nn.gelu(values_in, approximate=True)


def block_scores(query_part, key_part, query_pos, query_doc, key_pos, key_doc):
    scale = HD ** (-0.5)
    raw = (
        jnp.einsum("rhd,khd->hrk", query_part, key_part, preferred_element_type=jnp.float32) * scale
    )
    allowed = (key_pos[None, :] <= query_pos[:, None]) & (key_doc[None, :] == query_doc[:, None])
    return (raw, allowed[None])


def body(
    layer_input,
    first_values,
    segment_ids,
    pairing,
    norm_gains,
    norm_biases,
    w_qkv,
    w_out,
    w_up,
    w_down,
    cotangent,
):
    scale = HD ** (-0.5)
    ctx_index = lax.axis_index("ctx")
    local_rows = layer_input.shape[1]
    half_rows = local_rows // 2
    seq_length = local_rows * lax.axis_size("ctx")
    key_block = min(512, seq_length)
    key_count = seq_length // key_block
    offsets = jnp.arange(half_rows, dtype=jnp.int32)
    all_pos = (pairing[:, None] * half_rows + offsets[None, :]).reshape(seq_length)
    own_blocks = lax.dynamic_slice_in_dim(pairing, 2 * ctx_index, 2)
    own_pos = (own_blocks[:, None] * half_rows + offsets[None, :]).reshape(local_rows)
    doc_row = segment_ids[0]
    all_doc = jnp.take(doc_row, all_pos)
    own_doc = jnp.take(doc_row, own_pos)
    gathered = (
        lax.all_gather(norm_gains, "fsdp", axis=1, tiled=True),
        lax.all_gather(norm_biases, "fsdp", axis=1, tiled=True),
        lax.all_gather(w_qkv, "fsdp", axis=0, tiled=True),
        lax.all_gather(w_out, "fsdp", axis=0, tiled=True),
        lax.all_gather(w_up, "fsdp", axis=1, tiled=True),
        lax.all_gather(w_down, "fsdp", axis=0, tiled=True),
    )
    gains_all, biases_all, qkv_full, out_full, up_full, down_full = gathered
    gains = gains_all.astype(jnp.float32)
    biases = biases_all.astype(jnp.float32)
    inputs = layer_input[0].astype(jnp.float32)
    normed_one, norm_one_back = jax.vjp(norm_layer, inputs, gains[0], biases[0])
    h_one = normed_one.astype(jnp.bfloat16)
    qkv_low = jnp.dot(h_one, qkv_full, preferred_element_type=jnp.float32).astype(jnp.bfloat16)
    query_low = qkv_low[:, :D]
    key_low = qkv_low[:, D : 2 * D]
    fresh_low = qkv_low[:, 2 * D :]
    values_low = jnp.concatenate([fresh_low, first_values[0]], axis=1)
    keys_all, values_all = (
        lax.all_gather(key_low, "ctx", axis=0, tiled=True),
        lax.all_gather(values_low, "ctx", axis=0, tiled=True),
    )
    query_heads = query_low.reshape(local_rows, HEADS, HD)
    key_blocks = keys_all.reshape(key_count, key_block, HEADS, HD)
    value_blocks = values_all.reshape(key_count, key_block, HEADS, HD)
    pos_blocks = all_pos.reshape(key_count, key_block)
    doc_blocks = all_doc.reshape(key_count, key_block)

    def stats_step(carry, block):
        running_top, running_total = carry
        key_part, key_pos, key_doc = block
        raw, allowed = block_scores(query_heads, key_part, own_pos, own_doc, key_pos, key_doc)
        masked = jnp.where(allowed, raw, NEGATIVE)
        new_top = jnp.maximum(running_top, jnp.max(masked, axis=-1))
        terms = jnp.where(allowed, jnp.exp(raw - new_top[..., None]), 0.0)
        running_total = running_total * jnp.exp(running_top - new_top) + jnp.sum(terms, axis=-1)
        return ((new_top, running_total), None)

    start_top = jnp.full((HEADS, local_rows), NEGATIVE, jnp.float32)
    start_total = jnp.zeros((HEADS, local_rows), jnp.float32)
    (final_top, final_total), _ = lax.scan(
        stats_step, (start_top, start_total), (key_blocks, pos_blocks, doc_blocks)
    )
    log_total = final_top + jnp.log(final_total)

    def mix_step(accum, block):
        key_part, value_part, key_pos, key_doc = block
        raw, allowed = block_scores(query_heads, key_part, own_pos, own_doc, key_pos, key_doc)
        probs = jnp.where(allowed, jnp.exp(raw - log_total[..., None]), 0.0).astype(jnp.bfloat16)
        return (
            accum
            + jnp.einsum("hrk,khd->rhd", probs, value_part, preferred_element_type=jnp.float32),
            None,
        )

    mixed, _ = lax.scan(
        mix_step,
        jnp.zeros((local_rows, HEADS, HD), jnp.float32),
        (key_blocks, value_blocks, pos_blocks, doc_blocks),
    )
    attn_low = mixed.reshape(local_rows, D).astype(jnp.bfloat16)
    resid = inputs + jnp.dot(attn_low, out_full, preferred_element_type=jnp.float32)
    normed_two, norm_two_back = jax.vjp(norm_layer, resid, gains[1], biases[1])
    h_two = normed_two.astype(jnp.bfloat16)
    upper = jnp.dot(h_two, up_full, preferred_element_type=jnp.float32)
    active, gelu_back = jax.vjp(gelu_tanh, upper)
    active_low = active.astype(jnp.bfloat16)
    layer_out = (resid + jnp.dot(active_low, down_full, preferred_element_type=jnp.float32)).astype(
        jnp.bfloat16
    )
    regathered = (
        lax.all_gather(norm_gains, "fsdp", axis=1, tiled=True),
        lax.all_gather(norm_biases, "fsdp", axis=1, tiled=True),
        lax.all_gather(w_qkv, "fsdp", axis=0, tiled=True),
        lax.all_gather(w_out, "fsdp", axis=0, tiled=True),
        lax.all_gather(w_up, "fsdp", axis=1, tiled=True),
        lax.all_gather(w_down, "fsdp", axis=0, tiled=True),
    )
    qkv_back = regathered[2]
    out_back = regathered[3]
    up_back = regathered[4]
    down_back = regathered[5]
    cot_low = cotangent[0]
    cot_full = cot_low.astype(jnp.float32)
    down_grad = jnp.dot(active_low.T, cot_low, preferred_element_type=jnp.float32)
    dactive = jnp.dot(cot_low, down_back.T, preferred_element_type=jnp.float32)
    dupper_low = gelu_back(dactive)[0].astype(jnp.bfloat16)
    up_grad = jnp.dot(h_two.T, dupper_low, preferred_element_type=jnp.float32)
    dh_two = jnp.dot(dupper_low, up_back.T, preferred_element_type=jnp.float32)
    dresid_norm, gain_two_grad, bias_two_grad = norm_two_back(dh_two)
    dresid = cot_full + dresid_norm
    dbranch_low = dresid.astype(jnp.bfloat16)
    out_grad = jnp.dot(attn_low.T, dbranch_low, preferred_element_type=jnp.float32)
    dmixed_low = jnp.dot(dbranch_low, out_back.T, preferred_element_type=jnp.float32).astype(
        jnp.bfloat16
    )
    dmixed_heads = dmixed_low.reshape(local_rows, HEADS, HD)
    row_terms = jnp.sum(dmixed_heads.astype(jnp.float32) * mixed, axis=-1).T

    def grad_step(accum, block):
        key_part, value_part, key_pos, key_doc = block
        raw, allowed = block_scores(query_heads, key_part, own_pos, own_doc, key_pos, key_doc)
        probs = jnp.where(allowed, jnp.exp(raw - log_total[..., None]), 0.0)
        dprobs = jnp.einsum(
            "rhd,khd->hrk", dmixed_heads, value_part, preferred_element_type=jnp.float32
        )
        dscore_low = (probs * (dprobs - row_terms[..., None])).astype(jnp.bfloat16)
        accum = accum + jnp.einsum(
            "hrk,khd->rhd", dscore_low, key_part, preferred_element_type=jnp.float32
        )
        dkey_part = jnp.einsum(
            "hrk,rhd->khd", dscore_low, query_heads, preferred_element_type=jnp.float32
        )
        dvalue_part = jnp.einsum(
            "hrk,rhd->khd",
            probs.astype(jnp.bfloat16),
            dmixed_heads,
            preferred_element_type=jnp.float32,
        )
        return (accum, (dkey_part, dvalue_part))

    dquery_sum, (dkey_parts, dvalue_parts) = lax.scan(
        grad_step,
        jnp.zeros((local_rows, HEADS, HD), jnp.float32),
        (key_blocks, value_blocks, pos_blocks, doc_blocks),
    )
    dkeys_all = dkey_parts.reshape(seq_length, D) * scale
    dvalues_all = dvalue_parts.reshape(seq_length, D)
    own_dkeys, own_dvalues = (
        lax.psum_scatter(
            dkeys_all.astype(jnp.bfloat16), "ctx", scatter_dimension=0, tiled=True
        ).astype(jnp.float32),
        lax.psum_scatter(
            dvalues_all.astype(jnp.bfloat16), "ctx", scatter_dimension=0, tiled=True
        ).astype(jnp.float32),
    )
    dquery = dquery_sum.reshape(local_rows, D) * scale
    fresh_width = VH * HD
    first_grad = own_dvalues[:, fresh_width:]
    dqkv_low = jnp.concatenate(
        [
            dquery.astype(jnp.bfloat16),
            own_dkeys.astype(jnp.bfloat16),
            own_dvalues[:, :fresh_width].astype(jnp.bfloat16),
        ],
        axis=1,
    )
    qkv_grad = jnp.dot(h_one.T, dqkv_low, preferred_element_type=jnp.float32)
    dh_one = jnp.dot(dqkv_low, qkv_back.T, preferred_element_type=jnp.float32)
    dinput_norm, gain_one_grad, bias_one_grad = norm_one_back(dh_one)
    input_grad = dresid + dinput_norm
    gain_grads = jnp.stack([gain_one_grad, gain_two_grad])
    bias_grads = jnp.stack([bias_one_grad, bias_two_grad])
    shares = (
        lax.psum_scatter(
            gain_grads.astype(jnp.bfloat16), "fsdp", scatter_dimension=1, tiled=True
        ).astype(jnp.float32),
        lax.psum_scatter(
            bias_grads.astype(jnp.bfloat16), "fsdp", scatter_dimension=1, tiled=True
        ).astype(jnp.float32),
        lax.psum_scatter(
            qkv_grad.astype(jnp.bfloat16), "fsdp", scatter_dimension=0, tiled=True
        ).astype(jnp.float32),
        lax.psum_scatter(
            out_grad.astype(jnp.bfloat16), "fsdp", scatter_dimension=0, tiled=True
        ).astype(jnp.float32),
        lax.psum_scatter(
            up_grad.astype(jnp.bfloat16), "fsdp", scatter_dimension=1, tiled=True
        ).astype(jnp.float32),
        lax.psum_scatter(
            down_grad.astype(jnp.bfloat16), "fsdp", scatter_dimension=0, tiled=True
        ).astype(jnp.float32),
    )
    summed = (
        lax.psum(shares[0].astype(jnp.bfloat16), ("dp", "ctx")).astype(jnp.float32),
        lax.psum(shares[1].astype(jnp.bfloat16), ("dp", "ctx")).astype(jnp.float32),
        lax.psum(shares[2].astype(jnp.bfloat16), ("dp", "ctx")).astype(jnp.float32),
        lax.psum(shares[3].astype(jnp.bfloat16), ("dp", "ctx")).astype(jnp.float32),
        lax.psum(shares[4].astype(jnp.bfloat16), ("dp", "ctx")).astype(jnp.float32),
        lax.psum(shares[5].astype(jnp.bfloat16), ("dp", "ctx")).astype(jnp.float32),
    )
    return (
        layer_out[None],
        input_grad[None],
        first_grad[None],
        summed[0],
        summed[1],
        summed[2],
        summed[3],
        summed[4],
        summed[5],
    )


def solution(mesh):
    in_specs = (
        P(("dp", "fsdp"), "ctx", None),
        P(("dp", "fsdp"), "ctx", None),
        P(("dp", "fsdp"), None),
        P(),
        P(None, "fsdp"),
        P(None, "fsdp"),
        P("fsdp", None),
        P("fsdp", None),
        P(None, "fsdp"),
        P("fsdp", None),
        P(("dp", "fsdp"), "ctx", None),
    )
    out_specs = (
        P(("dp", "fsdp"), "ctx", None),
        P(("dp", "fsdp"), "ctx", None),
        P(("dp", "fsdp"), "ctx", None),
        P(None, "fsdp"),
        P(None, "fsdp"),
        P("fsdp", None),
        P("fsdp", None),
        P(None, "fsdp"),
        P("fsdp", None),
    )
    return jax.shard_map(body, mesh=mesh, in_specs=in_specs, out_specs=out_specs, check_vma=False)
```

profile of v0, /device:TPU:0, one launch (start us, length us, event | category | flops | bytes accessed | tf_op | source)
XLA Modules:
  0.0 874.5 jit_solution(13623779563315954214)
XLA Ops:
  8.0 6.3 all-gather
  14.3 5.5 all-gather.1
  23.6 16.1 %all-gather.9.cloned.1.call-done = bf16[768,1920]{1,0:T(8,128)(2,1)} async-done(((bf16[192,1920]{1,0:T(8,128)(2,1)}), bf16[768,1920]{1,0:T(8,128)(2,1)}) %all-gather.9.cloned.1.call-update) | async-done | bytes 2949136 | tf_op jit(solution)/shard_map/all_gather | solution.py:64
  39.7 4.0 convolution_convert_fusion.3
  51.7 11.8 %gather_fusion = s32[2048]{0:T(1024)S(1)} fusion(s32[2048]{0:T(1024)S(1)} %bitcast.284, s32[2048]{0:T(1024)S(1)} %broadcast_clamp_fusion), kind=kCustom, calls=%fused_computation | custom fusion | bytes 24576 | tf_op jit(solution)/shard_map/jit(_take)/gather | solution.py:59
  65.0 43.7 %all-gather.13.cloned.1.call-done = bf16[2048,768]{1,0:T(8,128)(2,1)} async-done(((bf16[512,768]{1,0:T(8,128)(2,1)}), bf16[2048,768]{1,0:T(8,128)(2,1)}) %all-gather.13.cloned.1.call-update) | async-done | bytes 3145744 | tf_op jit(solution)/shard_map/all_gather | solution.py:81
  108.7 4.7 copy.76
  113.4 6.3 reshape.387
  119.6 4.3 copy.80
  123.9 24.9 %while.39 = (s32[]{:T(128)}, f32[12,512]{1,0:T(8,128)S(1)}, f32[12,512]{1,0:T(8,128)S(1)}, s32[4,512]{1,0:T(4,128)S(1)}, s32[4,512]{1,0:T(4,128)S(1)}, /*index=5...) while((s32[]{:T(128)}, f32[12,512]{1,0:T(8,128)S(1)}, ...), condition=%wide.region_5.6_spmd.clone, body=%wide.region_2.5_spmd.clone.sunk | while | flops 425490944 | bytes 27867280 | solution.py:102
  148.8 24.2 %all-gather.11.cloned.1.call-done = bf16[2048,768]{1,0:T(8,128)(2,1)} async-done(((bf16[512,768]{1,0:T(8,128)(2,1)}), bf16[2048,768]{1,0:T(8,128)(2,1)}) %all-gather.11.cloned.1.call-update) | async-done | bytes 3145744 | tf_op jit(solution)/shard_map/all_gather | solution.py:82
  173.0 4.7 copy.75
  177.7 6.2 reshape.386
  183.9 4.4 copy.79
  188.3 23.0 %while.40 = (s32[]{:T(128)}, f32[512,12,64]{0,2,1:T(8,128)S(1)}, bf16[4,512,12,64]{1,3,2,0:T(8,128)(2,1)}, s32[4,512]{1,0:T(4,128)S(1)}, s32[4,512]{1,0:T(4,128)...) while((s32[]{:T(128)}, f32[512,12,64]{0,2,1:T(8,128)S(1)}, ...), condition=%wide.region_7.8_spmd.clone, body=%wide.region_6.7_spmd.clone.sunk | while | flops 819462656 | bytes 6078098 | solution.py:117
  188.9 5.2 bitcast_add_fusion.4
  194.5 5.2 bitcast_add_fusion.4
  200.1 5.5 bitcast_add_fusion.4
  206.0 5.3 bitcast_add_fusion.4
  216.2 13.3 %all-gather.17.cloned.1.call-done = bf16[768,3072]{1,0:T(8,128)(2,1)} async-done(((bf16[768,768]{1,0:T(8,128)(2,1)}), bf16[768,3072]{1,0:T(8,128)(2,1)}) %all-gather.17.cloned.1.call-update) | async-done | bytes 4718608 | tf_op jit(solution)/shard_map/all_gather | solution.py:66
  229.5 8.2 fusion.88
  237.7 30.7 %all-gather.19.cloned.1.call-done = bf16[3072,768]{1,0:T(8,128)(2,1)} async-done(((bf16[768,768]{1,0:T(8,128)(2,1)}), bf16[3072,768]{1,0:T(8,128)(2,1)}) %all-gather.19.cloned.1.call-update) | async-done | bytes 4718608 | tf_op jit(solution)/shard_map/all_gather | solution.py:67
  268.4 9.3 %fusion.58 = bf16[512,3072]{1,0:T(8,128)(2,1)S(1)} fusion(f32[512,3072]{1,0:T(8,128)} %fusion.88, bf16[3072,768]{1,0:T(8,128)(2,1)} %all-gather.19.cloned.1.call-done, bf16[1,512,768]{2,1,0:T(8,128)(2,1)S(1)} %copy-done.13), kind=kOutput, calls=%fused_computation.72 | convolution fusion | flops 2447376384 | bytes 14942208 | tf_op jit(solution)/shard_map/dot_general | solution.py:147
  287.0 88.2 %while.41 = (s32[]{:T(128)}, f32[512,12,64]{0,2,1:T(8,128)}, f32[4,512,12,64]{1,3,2,0:T(8,128)}, bf16[4,512,12,64]{1,3,2,0:T(8,128)(2,1)}, bf16[4,512,12,64]{1,3...) while((s32[]{:T(128)}, f32[512,12,64]{0,2,1:T(8,128)}, ...), condition=%wide.region_14.15_spmd.clone, body=%wide.region_13.14_spmd.clone.sunk | while | flops 2046296576 | bytes 81885488 | solution.py:183
  291.7 4.6 bitcast_dynamic-update-slice_fusion.5
  296.2 5.8 fusion.154
  313.3 4.6 bitcast_dynamic-update-slice_fusion.5
  317.8 5.8 fusion.154
  335.5 4.6 bitcast_dynamic-update-slice_fusion.5
  340.0 5.8 fusion.154
  357.6 4.6 bitcast_dynamic-update-slice_fusion.5
  362.2 5.8 fusion.154
  375.2 4.3 copy.85
  394.5 6.5 convolution_convert_fusion.1
  402.1 8.3 convolution_convert_fusion
  412.9 29.8 %reduce-scatter.15.cloned.1.call-done = bf16[512,768]{0,1:T(8,128)(2,1)} async-done(((bf16[2048,768]{0,1:T(8,128)(2,1)}), bf16[512,768]{0,1:T(8,128)(2,1)}) %reduce-scatter.15.cloned.1.call-update) | async-done | bytes 786448 | tf_op jit(solution)/shard_map/reduce_scatter | solution.py:194
  444.9 60.4 %reduce-scatter.13.cloned.1.call-done = bf16[512,768]{0,1:T(8,128)(2,1)} async-done(((bf16[2048,768]{0,1:T(8,128)(2,1)}), bf16[512,768]{0,1:T(8,128)(2,1)}) %reduce-scatter.13.cloned.1.call-update) | async-done | bytes 786448 | tf_op jit(solution)/shard_map/reduce_scatter | solution.py:191
  505.4 5.2 convolution_convert_fusion.2
  510.6 4.1 fusion.89
  518.9 15.4 %reduce-scatter.19.cloned.1.call-done = bf16[192,768]{1,0:T(8,128)(2,1)} async-done(((bf16[768,768]{1,0:T(8,128)(2,1)}), bf16[192,768]{1,0:T(8,128)(2,1)}) %reduce-scatter.19.cloned.1.call-update) | async-done | bytes 294928 | tf_op jit(solution)/shard_map/reduce_scatter | solution.py:225
  534.2 50.4 %reduce-scatter.21.cloned.1.call-done = bf16[768,768]{1,0:T(8,128)(2,1)} async-done(((bf16[768,3072]{1,0:T(8,128)(2,1)}), bf16[768,768]{1,0:T(8,128)(2,1)}) %reduce-scatter.21.cloned.1.call-update) | async-done | bytes 1179664 | tf_op jit(solution)/shard_map/reduce_scatter | solution.py:228
  584.7 50.4 %reduce-scatter.23.cloned.1.call-done = bf16[768,768]{1,0:T(8,128)(2,1)} async-done(((bf16[3072,768]{1,0:T(8,128)(2,1)}), bf16[768,768]{1,0:T(8,128)(2,1)}) %reduce-scatter.23.cloned.1.call-update) | async-done | bytes 1179664 | tf_op jit(solution)/shard_map/reduce_scatter | solution.py:231
  635.1 39.3 %reduce-scatter.17.cloned.1.call-done = bf16[192,1920]{1,0:T(8,128)(2,1)} async-done(((bf16[768,1920]{1,0:T(8,128)(2,1)}), bf16[192,1920]{1,0:T(8,128)(2,1)}) %reduce-scatter.17.cloned.1.call-update) | async-done | bytes 737296 | tf_op jit(solution)/shard_map/reduce_scatter | solution.py:222
  674.4 9.3 %fusion.72 = bf16[1,512,768]{2,1,0:T(8,128)(2,1)} fusion(f32[512,768]{1,0:T(8,128)} %copy-done.9, bf16[3072,768]{1,0:T(8,128)(2,1)} %all-gather.19.cloned.1.call-done, f32[512,3072]{1,0:T(8,128)} %fusion.88), kind=kOutput, calls=%fused_computation.108 | convolution fusion | flops 2430861312 | bytes 13369344 | tf_op jit(solution)/shard_map/dot_general | solution.py:129
  689.3 7.8 reduce-scatter.25.cloned.1.call-done
  698.1 21.2 %reduce-scatter.27.cloned.1.call-done = bf16[192,2]{1,0:T(8,128)(2,1)} async-done(((bf16[768,2]{1,0:T(8,128)(2,1)}), bf16[192,2]{1,0:T(8,128)(2,1)}) %reduce-scatter.27.cloned.1.call-update) | async-done | bytes 784
  720.1 22.1 %all-reduce = (bf16[2,192]{1,0:T(2,128)(2,1)S(1)}, bf16[2,192]{1,0:T(2,128)(2,1)S(1)}) all-reduce(bf16[2,192]{1,0:T(2,128)(2,1)S(1)} %copy.92, bf16[2,192]{1,0:T(2,128)(2,1)S(1)} %copy.94), channel_id=1, replica_groups=mesh['dp'=2,'ctx'=4,'fsdp'=4] {'dp','ctx'}, use_global_device_ids=true, to_apply=%region_22.23 | all-reduce | flops 768 | bytes 3072 | tf_op jit(solution)/shard_map/psum | solution.py:236
  743.4 116.9 %all-reduce.4.cloned.1.call-done = (bf16[192,1920]{1,0:T(8,128)(2,1)}, bf16[192,768]{1,0:T(8,128)(2,1)}, bf16[768,768]{1,0:T(8,128)(2,1)}, bf16[768,768]{1,0:T(8,128)(2,1)}) async-done(((bf16[192,1920]{1,0:T(8,128)(2,1)}, bf16[192,768]{1,0:T(8,128)(2,1)}, bf16[768,768]{1,0:T(8,128)(2,1)}, bf16[768,768]{1,0:T(8,128)(2,1)}), (bf16[192,1920]{1,0:T(8,128)(2,1)}, bf16[192,768]{1,0:T(8,128)(2,1)}, ...) | async-done | bytes 3391504 | tf_op jit(solution)/shard_map/psum | solution.py:238
  (296 shorter events, 141.3 us)
Async XLA Ops:
  7.2 41.4 %copy-start = (s32[1,2048]{1,0:T(1,128)S(1)}, s32[1,2048]{1,0:T(1,128)}, u32[]{:S(2)}) copy-start(s32[1,2048]{1,0:T(1,128)} %param.19) | copy-start | bytes 24580
  7.2 32.5 %all-gather.9.cloned.1.call-start = ((), (), s32[]{:S(2)}) async-start(), calls=%async_computation.8 | async-start | bytes 3686400 | tf_op jit(solution)/shard_map/all_gather | solution.py:64
  7.9 100.7 %all-gather.13.cloned.1.call-start = ((), (), s32[]{:S(2)}) async-start(), calls=%async_computation.10 | async-start | bytes 3932160 | tf_op jit(solution)/shard_map/all_gather | solution.py:81
  20.0 19.8 %copy-start.24 = (f32[768]{0:T(1024)}, f32[768]{0:T(1024)S(1)}, u32[]{:S(2)}) copy-start(f32[768]{0:T(1024)S(1)} %get-tuple-element.570) | copy-start | bytes 9220
  20.0 19.8 %copy-start.34 = (f32[768]{0:T(1024)}, f32[768]{0:T(1024)S(1)}, u32[]{:S(2)}) copy-start(f32[768]{0:T(1024)S(1)} %get-tuple-element.475) | copy-start | bytes 9220
  21.5 18.2 %copy-start.26 = (f32[512]{0:T(512)}, f32[512]{0:T(512)S(1)}, u32[]{:S(2)}) copy-start(f32[512]{0:T(512)S(1)} %broadcast_multiply_fusion.1) | copy-start | bytes 6148
  23.6 16.2 %copy-start.28 = (f32[512]{0:T(512)}, f32[512]{0:T(512)S(1)}, u32[]{:S(2)}) copy-start(f32[512]{0:T(512)S(1)} %fusion.81) | copy-start | bytes 6148
  45.0 3.1 copy-start.38
  45.0 128.0 %all-gather.11.cloned.1.call-start = ((), (), s32[]{:S(2)}) async-start(), calls=%async_computation.9 | async-start | bytes 3932160 | tf_op jit(solution)/shard_map/all_gather | solution.py:82
  46.1 166.2 %all-gather.15.cloned.1.call-start = ((), (), s32[]{:S(2)}) async-start(), calls=%async_computation.11 | async-start | bytes 1474560 | tf_op jit(solution)/shard_map/all_gather | solution.py:65
  46.7 182.8 %all-gather.17.cloned.1.call-start = ((), (), s32[]{:S(2)}) async-start(), calls=%async_computation.12 | async-start | bytes 5898240 | tf_op jit(solution)/shard_map/all_gather | solution.py:66
  47.3 221.1 %all-gather.19.cloned.1.call-start = ((), (), s32[]{:S(2)}) async-start(), calls=%async_computation.13 | async-start | bytes 5898240 | tf_op jit(solution)/shard_map/all_gather | solution.py:67
  47.8 394.9 %reduce-scatter.15.cloned.1.call-start = ((), (), s32[]{:S(2)}) async-start(), calls=%async_computation.15 | async-start | bytes 3932160 | tf_op jit(solution)/shard_map/reduce_scatter | solution.py:194
  188.3 24.0 %copy-start.7 = (bf16[1,512,768]{2,1,0:T(8,128)(2,1)S(1)}, bf16[1,512,768]{2,1,0:T(8,128)(2,1)}, u32[]{:S(2)}) copy-start(bf16[1,512,768]{2,1,0:T(8,128)(2,1)} %param.17) | copy-start | bytes 2359300
  229.5 38.9 %copy-start.13 = (bf16[1,512,768]{2,1,0:T(8,128)(2,1)S(1)}, bf16[1,512,768]{2,1,0:T(8,128)(2,1)}, u32[]{:S(2)}) copy-start(bf16[1,512,768]{2,1,0:T(8,128)(2,1)} %param.27) | copy-start | bytes 2359300
  268.4 9.3 %copy-start.10 = (f32[512,768]{1,0:T(8,128)S(1)}, f32[512,768]{1,0:T(8,128)}, u32[]{:S(2)}) copy-start(f32[512,768]{1,0:T(8,128)} %copy-done.9) | copy-start | bytes 4718596
  268.4 9.3 %copy-start.36 = (bf16[768,3072]{1,0:T(8,128)(2,1)S(1)}, bf16[768,3072]{1,0:T(8,128)(2,1)}, u32[]{:S(2)}) copy-start(bf16[768,3072]{1,0:T(8,128)(2,1)} %all-gather.17.cloned.1.call-done) | copy-start | bytes 14155780
  277.7 3.0 copy-start.39
  281.3 4.0 copy-start.30
  302.0 3.5 copy-start.3
  305.5 3.2 copy-start.16
  323.6 4.0 copy-start.3
  327.6 3.2 copy-start.16
  345.8 4.0 copy-start.3
  349.8 3.2 copy-start.16
  367.9 4.0 copy-start.3
  371.9 3.2 copy-start.16
  382.3 123.0 %reduce-scatter.13.cloned.1.call-start = ((), (), s32[]{:S(2)}) async-start(), calls=%async_computation.14 | async-start | bytes 3932160 | tf_op jit(solution)/shard_map/reduce_scatter | solution.py:191
  391.2 3.2 copy-start.11
  391.3 143.0 %reduce-scatter.19.cloned.1.call-start = ((), (), s32[]{:S(2)}) async-start(), calls=%async_computation.17 | async-start | bytes 1474560 | tf_op jit(solution)/shard_map/reduce_scatter | solution.py:225
  394.4 190.2 %reduce-scatter.21.cloned.1.call-start = ((), (), s32[]{:S(2)}) async-start(), calls=%async_computation.18 | async-start | bytes 5898240 | tf_op jit(solution)/shard_map/reduce_scatter | solution.py:228
  401.0 234.0 %reduce-scatter.23.cloned.1.call-start = ((), (), s32[]{:S(2)}) async-start(), calls=%async_computation.19 | async-start | bytes 5898240 | tf_op jit(solution)/shard_map/reduce_scatter | solution.py:231
  410.4 94.9 %copy-start.8 = (bf16[1,512,768]{2,1,0:T(8,128)(2,1)S(1)}, bf16[1,512,768]{2,1,0:T(8,128)(2,1)}, u32[]{:S(2)}) copy-start(bf16[1,512,768]{2,1,0:T(8,128)(2,1)} %param.17) | copy-start | bytes 2359300
  410.5 94.9 %copy-start.25 = (f32[768]{0:T(1024)S(1)}, f32[768]{0:T(1024)}, u32[]{:S(2)}) copy-start(f32[768]{0:T(1024)} %copy-done.24) | copy-start | bytes 9220
  410.5 94.9 %copy-start.27 = (f32[512]{0:T(512)S(1)}, f32[512]{0:T(512)}, u32[]{:S(2)}) copy-start(f32[512]{0:T(512)} %copy-done.26) | copy-start | bytes 6148
  410.5 94.8 %copy-start.29 = (f32[512]{0:T(512)S(1)}, f32[512]{0:T(512)}, u32[]{:S(2)}) copy-start(f32[512]{0:T(512)} %copy-done.28) | copy-start | bytes 6148
  410.5 94.8 %copy-start.35 = (f32[768]{0:T(1024)S(1)}, f32[768]{0:T(1024)}, u32[]{:S(2)}) copy-start(f32[768]{0:T(1024)} %copy-done.34) | copy-start | bytes 9220
  410.5 263.9 %reduce-scatter.17.cloned.1.call-start = ((), (), s32[]{:S(2)}) async-start(), calls=%async_computation.16 | async-start | bytes 3686400 | tf_op jit(solution)/shard_map/reduce_scatter | solution.py:222
  505.3 5.3 copy-start.22
  510.5 186.6 %reduce-scatter.25.cloned.1.call-start = ((), (), s32[]{:S(2)}) async-start(), calls=%async_computation.20 | async-start | bytes 245760
  510.6 4.1 copy-start.33
  517.6 201.6 %reduce-scatter.27.cloned.1.call-start = ((), (), s32[]{:S(2)}) async-start(), calls=%async_computation.21 | async-start | bytes 245760
  518.6 341.7 %all-reduce.4.cloned.1.call-start = ((), (), s32[]{:S(2)}) async-start(), calls=%async_computation.22 | async-start | bytes 6782976 | tf_op jit(solution)/shard_map/psum | solution.py:238
  674.4 11.7 %copy-start.6 = (f32[512,768]{1,0:T(8,128)S(1)}, f32[512,768]{1,0:T(8,128)}, u32[]{:S(2)}) copy-start(f32[512,768]{1,0:T(8,128)} %copy-done.5) | copy-start | bytes 4718596
  674.4 11.7 %copy-start.31 = (f32[512]{0:T(512)S(1)}, f32[512]{0:T(512)}, u32[]{:S(2)}) copy-start(f32[512]{0:T(512)} %copy-done.30) | copy-start | bytes 6148
  860.3 4.3 copy-start.18
  860.3 5.9 copy-start.17
  864.6 3.2 copy-start.1
  (19 other events, 22.3 us)
Sparse Core Ops, SparseCore 0:
  9.6 30.1 all-gather.8
  45.1 63.4 all-gather.12
  110.8 62.1 all-gather.10
  174.4 16.0 all-gather.14
  192.0 37.4 all-gather.16
  230.9 37.4 all-gather.18
  382.4 60.2 reduce-scatter.14
  445.0 60.2 reduce-scatter.12
  508.5 25.7 reduce-scatter.18
  536.8 47.8 reduce-scatter.20
  587.2 47.8 reduce-scatter.22
  637.6 36.7 reduce-scatter.16
  677.4 19.7 reduce-scatter.24
  699.5 19.7 reduce-scatter.26
  723.1 137.1 all-reduce.3
where the time goes:
time: 879 us; the launch traced here: 875 us
  waiting for transfers between devices  522 us (59%)
  matrix products  180 us (20%)
  local copies, waits for them, and re-layouts  80.6 us (9%)
  other arithmetic  41 us (5%)
  blocking collectives  33.8 us (4%)
  between operations  14.8 us (2%)
    psum x1, waiting for transfers between devices, body(): lax.psum(shares[2].astype(jnp.bfloat16), ('dp', 'ctx')).astype(jnp.float32)  117 us
    reduce_scatter x1, waiting for transfers between devices, body(): lax.psum_scatter(dkeys_all.astype(jnp.bfloat16), 'ctx', scatter_dimension...  60.4 us
    reduce_scatter x1, waiting for transfers between devices, body(): lax.psum_scatter(up_grad.astype(jnp.bfloat16), 'fsdp', scatter_dimension=...  50.4 us
    reduce_scatter x1, waiting for transfers between devices, body(): lax.psum_scatter(down_grad.astype(jnp.bfloat16), 'fsdp', scatter_dimensio...  50.4 us
    all_gather x1, waiting for transfers between devices, body(): lax.all_gather(key_low, 'ctx', axis=0, tiled=True)  43.7 us
    reduce_scatter x1, waiting for transfers between devices, body(): lax.psum_scatter(qkv_grad.astype(jnp.bfloat16), 'fsdp', scatter_dimension...  39.3 us
    unnamed x17, waiting for transfers between devices  31.5 us
    all_gather x1, waiting for transfers between devices, body(): lax.all_gather(w_down, 'fsdp', axis=0, tiled=True)  30.7 us
  transfers between devices with their start and end apart: 15, of which 14 were waited for; matrix products, arithmetic and copies ran while one was open for 19% of the time, Pallas kernels for 0%

commit v1 on v0

--- a/solution.py
+++ b/solution.py
@@ -233,7 +233,9 @@
         ).astype(jnp.float32),
     )
     summed = (
-        lax.psum(shares[0].astype(jnp.bfloat16), ("dp", "ctx")).astype(jnp.float32),
+        jnp.sum(lax.all_gather(shares[0].astype(jnp.bfloat16), ("dp", "ctx")), axis=0).astype(
+            jnp.float32
+        ),
         lax.psum(shares[1].astype(jnp.bfloat16), ("dp", "ctx")).astype(jnp.float32),
         lax.psum(shares[2].astype(jnp.bfloat16), ("dp", "ctx")).astype(jnp.float32),
         lax.psum(shares[3].astype(jnp.bfloat16), ("dp", "ctx")).astype(jnp.float32),

time: 879 us -> 879 us (level)
  blocking collectives: 33.8 us -> 54.4 us
  waiting for transfers between devices: 522 us -> 502 us
    unnamed x17, waiting for transfers between devices: 31.5 us -> 10.3 us
    all_gather x0 -> x1, blocking collectives: none -> 20.5 us  [body(): lax.all_gather(shares[0].astype(jnp.bfloat16), ('dp', 'ctx'))]
where the time goes in v1:
time: 879 us; the launch traced here: 874 us
  waiting for transfers between devices  502 us (57%)
  matrix products  180 us (20%)
  local copies, waits for them, and re-layouts  80.7 us (9%)
  blocking collectives  54.4 us (6%)
  other arithmetic  41 us (5%)
  between operations  14.8 us (2%)
    psum x1, waiting for transfers between devices, body(): lax.psum(shares[2].astype(jnp.bfloat16), ('dp', 'ctx')).astype(jnp.float32)  117 us
    reduce_scatter x1, waiting for transfers between devices, body(): lax.psum_scatter(dkeys_all.astype(jnp.bfloat16), 'ctx', scatter_dimension...  60.5 us
    reduce_scatter x1, waiting for transfers between devices, body(): lax.psum_scatter(up_grad.astype(jnp.bfloat16), 'fsdp', scatter_dimension=...  50.4 us
    reduce_scatter x1, waiting for transfers between devices, body(): lax.psum_scatter(down_grad.astype(jnp.bfloat16), 'fsdp', scatter_dimensio...  50.4 us
    all_gather x1, waiting for transfers between devices, body(): lax.all_gather(key_low, 'ctx', axis=0, tiled=True)  43.7 us
    reduce_scatter x1, waiting for transfers between devices, body(): lax.psum_scatter(qkv_grad.astype(jnp.bfloat16), 'fsdp', scatter_dimension...  39.3 us
    all_gather x1, waiting for transfers between devices, body(): lax.all_gather(w_down, 'fsdp', axis=0, tiled=True)  30.7 us
    reduce_scatter x1, waiting for transfers between devices, body(): lax.psum_scatter(dvalues_all.astype(jnp.bfloat16), 'ctx', scatter_dimensi...  29.8 us
  transfers between devices with their start and end apart: 15, of which 14 were waited for; matrix products, arithmetic and copies ran while one was open for 19% of the time, Pallas kernels for 0%

profile of v1, /device:TPU:0, one launch (start us, length us, event | category | flops | bytes accessed | tf_op | source)
XLA Modules:
  0.0 874.5 jit_solution(11011141911040499158)
XLA Ops:
  8.0 6.3 all-gather.1
  14.3 5.5 all-gather.2
  23.6 16.1 %all-gather.11.cloned.1.call-done = bf16[768,1920]{1,0:T(8,128)(2,1)} async-done(((bf16[192,1920]{1,0:T(8,128)(2,1)}), bf16[768,1920]{1,0:T(8,128)(2,1)}) %all-gather.11.cloned.1.call-update) | async-done | bytes 2949136 | tf_op jit(solution)/shard_map/all_gather | solution.py:64
  39.7 4.0 convolution_convert_fusion.3
  51.7 11.8 %gather_fusion = s32[2048]{0:T(1024)S(1)} fusion(s32[2048]{0:T(1024)S(1)} %bitcast.285, s32[2048]{0:T(1024)S(1)} %broadcast_clamp_fusion), kind=kCustom, calls=%fused_computation | custom fusion | bytes 24576 | tf_op jit(solution)/shard_map/jit(_take)/gather | solution.py:59
  65.0 43.7 %all-gather.15.cloned.1.call-done = bf16[2048,768]{1,0:T(8,128)(2,1)} async-done(((bf16[512,768]{1,0:T(8,128)(2,1)}), bf16[2048,768]{1,0:T(8,128)(2,1)}) %all-gather.15.cloned.1.call-update) | async-done | bytes 3145744 | tf_op jit(solution)/shard_map/all_gather | solution.py:81
  108.7 4.7 copy.76
  113.4 6.3 reshape.387
  119.6 4.3 copy.80
  123.9 24.9 %while.39 = (s32[]{:T(128)}, f32[12,512]{1,0:T(8,128)S(1)}, f32[12,512]{1,0:T(8,128)S(1)}, s32[4,512]{1,0:T(4,128)S(1)}, s32[4,512]{1,0:T(4,128)S(1)}, /*index=5...) while((s32[]{:T(128)}, f32[12,512]{1,0:T(8,128)S(1)}, ...), condition=%wide.region_5.6_spmd.clone, body=%wide.region_2.5_spmd.clone.sunk | while | flops 425490944 | bytes 27867280 | solution.py:102
  148.8 24.2 %all-gather.13.cloned.1.call-done = bf16[2048,768]{1,0:T(8,128)(2,1)} async-done(((bf16[512,768]{1,0:T(8,128)(2,1)}), bf16[2048,768]{1,0:T(8,128)(2,1)}) %all-gather.13.cloned.1.call-update) | async-done | bytes 3145744 | tf_op jit(solution)/shard_map/all_gather | solution.py:82
  173.0 4.7 copy.75
  177.7 6.3 reshape.386
  184.0 4.4 copy.79
  188.3 23.0 %while.40 = (s32[]{:T(128)}, f32[512,12,64]{0,2,1:T(8,128)S(1)}, bf16[4,512,12,64]{1,3,2,0:T(8,128)(2,1)}, s32[4,512]{1,0:T(4,128)S(1)}, s32[4,512]{1,0:T(4,128)...) while((s32[]{:T(128)}, f32[512,12,64]{0,2,1:T(8,128)S(1)}, ...), condition=%wide.region_7.8_spmd.clone, body=%wide.region_6.7_spmd.clone.sunk | while | flops 819462656 | bytes 6078098 | solution.py:117
  188.9 5.2 bitcast_add_fusion.4
  194.6 5.2 bitcast_add_fusion.4
  200.2 5.5 bitcast_add_fusion.4
  206.0 5.3 bitcast_add_fusion.4
  216.2 13.3 %all-gather.19.cloned.1.call-done = bf16[768,3072]{1,0:T(8,128)(2,1)} async-done(((bf16[768,768]{1,0:T(8,128)(2,1)}), bf16[768,3072]{1,0:T(8,128)(2,1)}) %all-gather.19.cloned.1.call-update) | async-done | bytes 4718608 | tf_op jit(solution)/shard_map/all_gather | solution.py:66
  229.5 8.2 fusion.88
  237.7 30.7 %all-gather.21.cloned.1.call-done = bf16[3072,768]{1,0:T(8,128)(2,1)} async-done(((bf16[768,768]{1,0:T(8,128)(2,1)}), bf16[3072,768]{1,0:T(8,128)(2,1)}) %all-gather.21.cloned.1.call-update) | async-done | bytes 4718608 | tf_op jit(solution)/shard_map/all_gather | solution.py:67
  268.4 9.3 %fusion.58 = bf16[512,3072]{1,0:T(8,128)(2,1)S(1)} fusion(f32[512,3072]{1,0:T(8,128)} %fusion.88, bf16[3072,768]{1,0:T(8,128)(2,1)} %all-gather.21.cloned.1.call-done, bf16[1,512,768]{2,1,0:T(8,128)(2,1)S(1)} %copy-done.13), kind=kOutput, calls=%fused_computation.72 | convolution fusion | flops 2447376384 | bytes 14942208 | tf_op jit(solution)/shard_map/dot_general | solution.py:147
  287.0 88.2 %while.41 = (s32[]{:T(128)}, f32[512,12,64]{0,2,1:T(8,128)}, f32[4,512,12,64]{1,3,2,0:T(8,128)}, bf16[4,512,12,64]{1,3,2,0:T(8,128)(2,1)}, bf16[4,512,12,64]{1,3...) while((s32[]{:T(128)}, f32[512,12,64]{0,2,1:T(8,128)}, ...), condition=%wide.region_14.15_spmd.clone, body=%wide.region_13.14_spmd.clone.sunk | while | flops 2046296576 | bytes 81885488 | solution.py:183
  291.7 4.6 bitcast_dynamic-update-slice_fusion.5
  296.2 5.8 fusion.154
  313.3 4.6 bitcast_dynamic-update-slice_fusion.5
  317.8 5.8 fusion.154
  335.5 4.6 bitcast_dynamic-update-slice_fusion.5
  340.1 5.8 fusion.154
  357.6 4.5 bitcast_dynamic-update-slice_fusion.5
  362.2 5.8 fusion.154
  375.2 4.3 copy.85
  394.5 6.5 convolution_convert_fusion.1
  402.1 8.3 convolution_convert_fusion
  412.9 29.8 %reduce-scatter.15.cloned.1.call-done = bf16[512,768]{0,1:T(8,128)(2,1)} async-done(((bf16[2048,768]{0,1:T(8,128)(2,1)}), bf16[512,768]{0,1:T(8,128)(2,1)}) %reduce-scatter.15.cloned.1.call-update) | async-done | bytes 786448 | tf_op jit(solution)/shard_map/reduce_scatter | solution.py:194
  444.8 60.5 %reduce-scatter.13.cloned.1.call-done = bf16[512,768]{0,1:T(8,128)(2,1)} async-done(((bf16[2048,768]{0,1:T(8,128)(2,1)}), bf16[512,768]{0,1:T(8,128)(2,1)}) %reduce-scatter.13.cloned.1.call-update) | async-done | bytes 786448 | tf_op jit(solution)/shard_map/reduce_scatter | solution.py:191
  505.3 5.2 convolution_convert_fusion.2
  510.6 4.1 fusion.89
  518.8 15.4 %reduce-scatter.19.cloned.1.call-done = bf16[192,768]{1,0:T(8,128)(2,1)} async-done(((bf16[768,768]{1,0:T(8,128)(2,1)}), bf16[192,768]{1,0:T(8,128)(2,1)}) %reduce-scatter.19.cloned.1.call-update) | async-done | bytes 294928 | tf_op jit(solution)/shard_map/reduce_scatter | solution.py:225
  534.2 50.4 %reduce-scatter.21.cloned.1.call-done = bf16[768,768]{1,0:T(8,128)(2,1)} async-done(((bf16[768,3072]{1,0:T(8,128)(2,1)}), bf16[768,768]{1,0:T(8,128)(2,1)}) %reduce-scatter.21.cloned.1.call-update) | async-done | bytes 1179664 | tf_op jit(solution)/shard_map/reduce_scatter | solution.py:228
  584.6 50.4 %reduce-scatter.23.cloned.1.call-done = bf16[768,768]{1,0:T(8,128)(2,1)} async-done(((bf16[3072,768]{1,0:T(8,128)(2,1)}), bf16[768,768]{1,0:T(8,128)(2,1)}) %reduce-scatter.23.cloned.1.call-update) | async-done | bytes 1179664 | tf_op jit(solution)/shard_map/reduce_scatter | solution.py:231
  635.0 39.3 %reduce-scatter.17.cloned.1.call-done = bf16[192,1920]{1,0:T(8,128)(2,1)} async-done(((bf16[768,1920]{1,0:T(8,128)(2,1)}), bf16[192,1920]{1,0:T(8,128)(2,1)}) %reduce-scatter.17.cloned.1.call-update) | async-done | bytes 737296 | tf_op jit(solution)/shard_map/reduce_scatter | solution.py:222
  674.4 9.3 %fusion.72 = bf16[1,512,768]{2,1,0:T(8,128)(2,1)} fusion(f32[512,768]{1,0:T(8,128)} %copy-done.9, bf16[3072,768]{1,0:T(8,128)(2,1)} %all-gather.21.cloned.1.call-done, f32[512,3072]{1,0:T(8,128)} %fusion.88), kind=kOutput, calls=%fused_computation.108 | convolution fusion | flops 2430861312 | bytes 13369344 | tf_op jit(solution)/shard_map/dot_general | solution.py:129
  689.3 7.8 reduce-scatter.25.cloned.1.call-done
  698.0 20.5 %all-gather.3 = bf16[8,2,192]{2,1,0:T(2,128)(2,1)S(1)} all-gather(bf16[1,2,192]{2,1,0:T(2,128)(2,1)S(1)} %bitcast.323), channel_id=2, replica_groups=mesh['dp'=2,'ctx'=4,'fsdp'=4] {'dp','ctx'}, dimensions={0}, use_global_device_ids=true | all-gather | bytes 6912 | tf_op jit(solution)/shard_map/all_gather | solution.py:236
  720.1 22.1 %psum.35 = bf16[2,192]{1,0:T(2,128)(2,1)S(1)} all-reduce(bf16[2,192]{1,0:T(2,128)(2,1)S(1)} %copy.94), channel_id=1, replica_groups=mesh['dp'=2,'ctx'=4,'fsdp'=4] {'dp','ctx'}, use_global_device_ids=true, to_apply=%region_26.27 | all-reduce | flops 384 | bytes 1536 | tf_op jit(solution)/shard_map/psum | solution.py:239
  742.8 117.5 %all-reduce.3.cloned.1.call-done = (bf16[192,1920]{1,0:T(8,128)(2,1)}, bf16[192,768]{1,0:T(8,128)(2,1)}, bf16[768,768]{1,0:T(8,128)(2,1)}, bf16[768,768]{1,0:T(8,128)(2,1)}) async-done(((bf16[192,1920]{1,0:T(8,128)(2,1)}, bf16[192,768]{1,0:T(8,128)(2,1)}, bf16[768,768]{1,0:T(8,128)(2,1)}, bf16[768,768]{1,0:T(8,128)(2,1)}), (bf16[192,1920]{1,0:T(8,128)(2,1)}, bf16[192,768]{1,0:T(8,128)(2,1)}, ...) | async-done | bytes 3391504 | tf_op jit(solution)/shard_map/psum | solution.py:240
  (298 shorter events, 141.4 us)
Async XLA Ops:
  7.2 41.4 %copy-start = (s32[1,2048]{1,0:T(1,128)S(1)}, s32[1,2048]{1,0:T(1,128)}, u32[]{:S(2)}) copy-start(s32[1,2048]{1,0:T(1,128)} %param.19) | copy-start | bytes 24580
  7.2 32.5 %all-gather.11.cloned.1.call-start = ((), (), s32[]{:S(2)}) async-start(), calls=%async_computation.8 | async-start | bytes 3686400 | tf_op jit(solution)/shard_map/all_gather | solution.py:64
  7.9 100.7 %all-gather.15.cloned.1.call-start = ((), (), s32[]{:S(2)}) async-start(), calls=%async_computation.10 | async-start | bytes 3932160 | tf_op jit(solution)/shard_map/all_gather | solution.py:81
  20.0 19.8 %copy-start.24 = (f32[768]{0:T(1024)}, f32[768]{0:T(1024)S(1)}, u32[]{:S(2)}) copy-start(f32[768]{0:T(1024)S(1)} %get-tuple-element.568) | copy-start | bytes 9220
  20.0 19.8 %copy-start.34 = (f32[768]{0:T(1024)}, f32[768]{0:T(1024)S(1)}, u32[]{:S(2)}) copy-start(f32[768]{0:T(1024)S(1)} %get-tuple-element.475) | copy-start | bytes 9220
  21.5 18.2 %copy-start.26 = (f32[512]{0:T(512)}, f32[512]{0:T(512)S(1)}, u32[]{:S(2)}) copy-start(f32[512]{0:T(512)S(1)} %broadcast_multiply_fusion.1) | copy-start | bytes 6148
  23.6 16.1 %copy-start.28 = (f32[512]{0:T(512)}, f32[512]{0:T(512)S(1)}, u32[]{:S(2)}) copy-start(f32[512]{0:T(512)S(1)} %fusion.81) | copy-start | bytes 6148
  45.0 3.1 copy-start.38
  45.0 128.0 %all-gather.13.cloned.1.call-start = ((), (), s32[]{:S(2)}) async-start(), calls=%async_computation.9 | async-start | bytes 3932160 | tf_op jit(solution)/shard_map/all_gather | solution.py:82
  46.1 166.2 %all-gather.17.cloned.1.call-start = ((), (), s32[]{:S(2)}) async-start(), calls=%async_computation.11 | async-start | bytes 1474560 | tf_op jit(solution)/shard_map/all_gather | solution.py:65
  46.7 182.8 %all-gather.19.cloned.1.call-start = ((), (), s32[]{:S(2)}) async-start(), calls=%async_computation.12 | async-start | bytes 5898240 | tf_op jit(solution)/shard_map/all_gather | solution.py:66
  47.3 221.2 %all-gather.21.cloned.1.call-start = ((), (), s32[]{:S(2)}) async-start(), calls=%async_computation.13 | async-start | bytes 5898240 | tf_op jit(solution)/shard_map/all_gather | solution.py:67
  47.8 394.8 %reduce-scatter.15.cloned.1.call-start = ((), (), s32[]{:S(2)}) async-start(), calls=%async_computation.15 | async-start | bytes 3932160 | tf_op jit(solution)/shard_map/reduce_scatter | solution.py:194
  188.3 24.0 %copy-start.7 = (bf16[1,512,768]{2,1,0:T(8,128)(2,1)S(1)}, bf16[1,512,768]{2,1,0:T(8,128)(2,1)}, u32[]{:S(2)}) copy-start(bf16[1,512,768]{2,1,0:T(8,128)(2,1)} %param.17) | copy-start | bytes 2359300
  229.5 38.9 %copy-start.13 = (bf16[1,512,768]{2,1,0:T(8,128)(2,1)S(1)}, bf16[1,512,768]{2,1,0:T(8,128)(2,1)}, u32[]{:S(2)}) copy-start(bf16[1,512,768]{2,1,0:T(8,128)(2,1)} %param.27) | copy-start | bytes 2359300
  268.4 9.3 %copy-start.10 = (f32[512,768]{1,0:T(8,128)S(1)}, f32[512,768]{1,0:T(8,128)}, u32[]{:S(2)}) copy-start(f32[512,768]{1,0:T(8,128)} %copy-done.9) | copy-start | bytes 4718596
  268.4 9.3 %copy-start.36 = (bf16[768,3072]{1,0:T(8,128)(2,1)S(1)}, bf16[768,3072]{1,0:T(8,128)(2,1)}, u32[]{:S(2)}) copy-start(bf16[768,3072]{1,0:T(8,128)(2,1)} %all-gather.19.cloned.1.call-done) | copy-start | bytes 14155780
  277.7 3.0 copy-start.39
  281.3 4.0 copy-start.30
  302.0 3.5 copy-start.3
  305.5 3.2 copy-start.16
  323.6 4.0 copy-start.3
  327.6 3.3 copy-start.16
  345.8 4.0 copy-start.3
  349.8 3.2 copy-start.16
  367.9 4.0 copy-start.3
  371.9 3.2 copy-start.16
  382.3 123.0 %reduce-scatter.13.cloned.1.call-start = ((), (), s32[]{:S(2)}) async-start(), calls=%async_computation.14 | async-start | bytes 3932160 | tf_op jit(solution)/shard_map/reduce_scatter | solution.py:191
  391.2 3.2 copy-start.11
  391.3 143.0 %reduce-scatter.19.cloned.1.call-start = ((), (), s32[]{:S(2)}) async-start(), calls=%async_computation.17 | async-start | bytes 1474560 | tf_op jit(solution)/shard_map/reduce_scatter | solution.py:225
  394.4 190.2 %reduce-scatter.21.cloned.1.call-start = ((), (), s32[]{:S(2)}) async-start(), calls=%async_computation.18 | async-start | bytes 5898240 | tf_op jit(solution)/shard_map/reduce_scatter | solution.py:228
  401.0 234.0 %reduce-scatter.23.cloned.1.call-start = ((), (), s32[]{:S(2)}) async-start(), calls=%async_computation.19 | async-start | bytes 5898240 | tf_op jit(solution)/shard_map/reduce_scatter | solution.py:231
  410.4 94.9 %copy-start.8 = (bf16[1,512,768]{2,1,0:T(8,128)(2,1)S(1)}, bf16[1,512,768]{2,1,0:T(8,128)(2,1)}, u32[]{:S(2)}) copy-start(bf16[1,512,768]{2,1,0:T(8,128)(2,1)} %param.17) | copy-start | bytes 2359300
  410.4 94.9 %copy-start.25 = (f32[768]{0:T(1024)S(1)}, f32[768]{0:T(1024)}, u32[]{:S(2)}) copy-start(f32[768]{0:T(1024)} %copy-done.24) | copy-start | bytes 9220
  410.4 94.9 %copy-start.27 = (f32[512]{0:T(512)S(1)}, f32[512]{0:T(512)}, u32[]{:S(2)}) copy-start(f32[512]{0:T(512)} %copy-done.26) | copy-start | bytes 6148
  410.5 94.8 %copy-start.29 = (f32[512]{0:T(512)S(1)}, f32[512]{0:T(512)}, u32[]{:S(2)}) copy-start(f32[512]{0:T(512)} %copy-done.28) | copy-start | bytes 6148
  410.5 94.8 %copy-start.35 = (f32[768]{0:T(1024)S(1)}, f32[768]{0:T(1024)}, u32[]{:S(2)}) copy-start(f32[768]{0:T(1024)} %copy-done.34) | copy-start | bytes 9220
  410.5 263.9 %reduce-scatter.17.cloned.1.call-start = ((), (), s32[]{:S(2)}) async-start(), calls=%async_computation.16 | async-start | bytes 3686400 | tf_op jit(solution)/shard_map/reduce_scatter | solution.py:222
  505.3 5.3 copy-start.22
  510.5 186.6 %reduce-scatter.25.cloned.1.call-start = ((), (), s32[]{:S(2)}) async-start(), calls=%async_computation.20 | async-start | bytes 245760
  510.6 4.1 copy-start.33
  517.6 201.6 %reduce-scatter.27.cloned.1.call-start = ((), (), s32[]{:S(2)}) async-start(), calls=%async_computation.21 | async-start | bytes 245760
  518.5 341.7 %all-reduce.3.cloned.1.call-start = ((), (), s32[]{:S(2)}) async-start(), calls=%async_computation.22 | async-start | bytes 6782976 | tf_op jit(solution)/shard_map/psum | solution.py:240
  674.4 11.7 %copy-start.6 = (f32[512,768]{1,0:T(8,128)S(1)}, f32[512,768]{1,0:T(8,128)}, u32[]{:S(2)}) copy-start(f32[512,768]{1,0:T(8,128)} %copy-done.5) | copy-start | bytes 4718596
  674.4 11.7 %copy-start.31 = (f32[512]{0:T(512)S(1)}, f32[512]{0:T(512)}, u32[]{:S(2)}) copy-start(f32[512]{0:T(512)} %copy-done.30) | copy-start | bytes 6148
  860.2 4.3 copy-start.18
  860.3 5.9 copy-start.17
  864.5 3.2 copy-start.1
  (19 other events, 22.4 us)
Sparse Core Ops, SparseCore 0:
  9.6 30.1 all-gather.10
  45.1 63.4 all-gather.14
  110.8 62.1 all-gather.12
  174.4 16.0 all-gather.16
  192.0 37.4 all-gather.18
  230.9 37.4 all-gather.20
  382.4 60.2 reduce-scatter.14
  445.0 60.2 reduce-scatter.12
  508.4 25.7 reduce-scatter.18
  536.8 47.8 reduce-scatter.20
  587.2 47.8 reduce-scatter.22
  637.6 36.7 reduce-scatter.16
  677.4 19.7 reduce-scatter.24
  699.5 19.7 reduce-scatter.26
  723.1 137.1 all-reduce.2
